TPU v7x, 512 devices: a whole 4x4x16 slice. The times are simulated.
512 devices in a mesh: grid: 64 (over y, z), state: 8 (over x, core).
Axes of the slice: x: 4, y: 4, z: 16, core: 2. Of those that a mesh axis runs over, the one named last changes fastest.
Arguments:
- orbitals: float32 [8, 512, 64, 128], P('state', 'grid'), may hold values from -6 to 6
- potential: float32 [512, 64, 128], P('grid'), may hold values from 0 to 2
Outputs:
- corrections: float32 [8, 512, 64, 128], P('state', 'grid')
- correlation_gram: float32 [8, 8], P('state')
All inputs are finite; a program needn't handle non-finite values.
Results may differ from a plain program's by a relative error of at most 0.00095.
Values may be sent and summed in bfloat16 or wider, within the bound.
A program may use at most 64 MiB of HBM per device.

v0:
```python
import jax
import jax.numpy as jnp
from jax import lax
from jax.sharding import PartitionSpec as P

LEVELS = 4
COARSE_SWEEPS = 3
CENTER = -2.5
NEAR_COEF = 4.0 / 3.0
FAR_COEF = -1.0 / 12.0
SHIFT_TERM = 0.25
DAMPING = 2.0 / 3.0


def with_halo(block, sides, width):
    for axis, dim in sides:
        count = lax.axis_size(axis)
        forward = [(i, i + 1) for i in range(count - 1)]
        forward.append((count - 1, 0))
        backward = [(target, source) for source, target in forward]
        low = lax.ppermute(
            lax.slice_in_dim(block, block.shape[dim] - width, None, axis=dim), axis, forward
        )
        high = lax.ppermute(lax.slice_in_dim(block, 0, width, axis=dim), axis, backward)
        block = jnp.concatenate([low, block, high], axis=dim)
    return block


def laplace_four(values, axis):
    near = jnp.roll(values, 1, axis) + jnp.roll(values, -1, axis)
    far = jnp.roll(values, 2, axis) + jnp.roll(values, -2, axis)
    return CENTER * values + NEAR_COEF * near + FAR_COEF * far


def face_halo(values):
    return with_halo(values.astype(jnp.bfloat16), (("grid", 1),), 1).astype(values.dtype)


def level_apply(values, padded, inverse):
    beside = padded[:, 2:] + padded[:, :-2]
    beside = beside + jnp.roll(values, 1, 2) + jnp.roll(values, -1, 2)
    beside = beside + jnp.roll(values, 1, 3) + jnp.roll(values, -1, 3)
    return (SHIFT_TERM + 3.0 * inverse) * values - 0.5 * inverse * beside


def restrict(values):
    count, sx, sy, sz = values.shape
    shaped = values.reshape(count, sx // 2, 2, sy // 2, 2, sz // 2, 2)
    return jnp.mean(shaped, axis=(2, 4, 6))


def prolong(values):
    return jnp.repeat(jnp.repeat(jnp.repeat(values, 2, 1), 2, 2), 2, 3)


def jacobi_sweep(iterate, source, inverse, padder):
    diagonal = SHIFT_TERM + 3.0 * inverse
    applied = level_apply(iterate, padder(iterate), inverse)
    return iterate + DAMPING * (source - applied) / diagonal


def coarse_solve(source, inverse, padder):
    diagonal = SHIFT_TERM + 3.0 * inverse
    iterate = DAMPING * source / diagonal
    for repeat in range(COARSE_SWEEPS - 1):
        iterate = jacobi_sweep(iterate, source, inverse, padder)
    return iterate


def vcycle(source, depth_level):
    inverse = 0.25**depth_level
    diagonal = SHIFT_TERM + 3.0 * inverse
    if depth_level == LEVELS - 1:
        return coarse_solve(source, inverse, face_halo)
    iterate = DAMPING * source / diagonal
    remainder = source - level_apply(iterate, face_halo(iterate), inverse)
    coarse_error = vcycle(restrict(remainder), depth_level + 1)
    iterate = iterate + prolong(coarse_error)
    return jacobi_sweep(iterate, source, inverse, face_halo)


def on_device(orbitals, potential):
    padded = with_halo(orbitals, (("grid", 1),), 2)
    near = padded[:, 3:-1] + padded[:, 1:-3]
    far = padded[:, 4:] + padded[:, :-4]
    lap_first = CENTER * orbitals + NEAR_COEF * near + FAR_COEF * far
    lap = lap_first + laplace_four(orbitals, 2) + laplace_four(orbitals, 3)
    hpsi = -0.5 * lap + potential[None] * orbitals
    numer, denom = lax.psum(
        (jnp.sum(orbitals * hpsi, axis=(1, 2, 3)), jnp.sum(orbitals * orbitals, axis=(1, 2, 3))),
        "grid",
    )
    energy = numer / denom
    residual = hpsi - energy[:, None, None, None] * orbitals
    corrections = vcycle(residual, 0)
    count = corrections.shape[0]
    rounded = corrections.astype(jnp.bfloat16).reshape(count, -1)
    row_block = jnp.einsum(
        "ac,bc->ab",
        rounded,
        lax.all_gather(rounded, "state", axis=0, tiled=True),
        preferred_element_type=jnp.float32,
    )
    summed = lax.psum(row_block, "grid")
    correlation_gram = summed / jnp.float32(rounded.shape[1] * lax.axis_size("grid"))
    return (corrections, correlation_gram)


def solution(mesh):
    placed = (P("state", "grid", None, None), P("grid", None, None))
    return jax.shard_map(
        on_device,
        mesh=mesh,
        in_specs=placed,
        out_specs=(P("state", "grid", None, None), P("state", None)),
        check_vma=False,
    )
```

profile of v0, /device:TPU:4, one launch (start us, length us, event | category | flops | bytes accessed | tf_op | source)
XLA Modules:
  0.0 495.5 jit_solution(615986933523737960)
XLA Ops:
  7.2 1.5 fusion.122
  8.7 3.8 collective-permute-start.1
  12.5 11.9 %collective-permute-start = (f32[1,2,64,128]{3,2,1,0:T(8,128)}, f32[1,2,64,128]{3,2,1,0:T(8,128)S(1)}, u32[]{:S(2)}, u32[]{:S(2)}) collective-permute-start(f32[1,2,64,128]{3,2,1,0:T(8,128)} %get-tuple-element.64), channel_id=1, source_target_pairs={{8,0},{16,8},{24,16},{32,24},{40,32},{48,40},{56,48},{64,56},{72,6... | collective-permute-start | bytes 196616 | tf_op jit(solution)/shard_map/ppermute | solution.py:24
  24.5 0.8 fusion.123
  25.3 0.8 fusion.124
  26.1 1.2 copy.115
  27.3 1.0 fusion.117
  28.3 1.0 fusion.115
  29.3 1.2 fusion.113
  30.5 1.1 fusion.112
  31.7 0.6 fusion.114
  32.3 0.3 copy.125
  32.5 0.3 copy.121
  32.8 0.3 copy.127
  33.1 0.3 copy.123
  33.3 1.0 copy.136
  34.3 0.7 multiply_reduce_fusion.1
  35.1 1.0 copy.154
  36.1 0.8 fusion.119
  36.9 2.0 copy.153
  38.9 1.0 copy.155
  39.9 1.0 copy.156
  40.9 4.4 multiply_reduce_fusion
  45.3 140.7 %all-reduce = (f32[1]{0:T(128)}, f32[1]{0:T(128)}) all-reduce(f32[1]{0:T(128)} %bitcast.1, f32[1]{0:T(128)} %bitcast.2), channel_id=1, replica_groups=mesh['grid'=64,'state'=8] {'grid'}, use_global_device_ids=true, to_apply=%region_1.2 | all-reduce | flops 2 | bytes 16 | tf_op jit(solution)/shard_map/psum | solution.py:89
  187.7 0.2 fusion.111
  188.0 1.9 collective-permute-start.2
  190.0 7.2 %collective-permute-start.3 = (bf16[1,1,64,128]{2,1,3,0:T(2,128)(2,1)S(1)}, bf16[1,1,64,128]{2,1,3,0:T(2,128)(2,1)S(1)}, u32[]{:S(2)}, u32[]{:S(2)}) collective-permute-start(bf16[1,1,64,128]{2,1,3,0:T(2,128)(2,1)S(1)} %get-tuple-element.59), channel_id=1, source_target_pairs={{8,0},{16,8},{24,16},{32,24},{40,32},{48,40},{56,48},{64,56},{72,6... | collective-permute-start | bytes 49160 | tf_op jit(solution)/shard_map/ppermute | solution.py:24
  197.2 0.3 collective-permute-done.2
  197.5 1.6 collective-permute-done.3
  199.1 0.3 maximum_convert_fusion
  199.4 0.5 fusion.18
  200.1 18.1 %reshape.809 = f32[4,2,32,2,64,2]{5,4,3,2,1,0:T(8,128)} reshape(f32[1,8,64,128]{3,2,1,0:T(8,128)S(1)} %copy.140) | data formatting | bytes 524288 | tf_op jit(solution)/shard_map/reshape | solution.py:48
  218.2 7.0 %reduce_sum.60 = f32[4,32,64]{2,1,0:T(8,128)S(1)} reduce(f32[4,2,32,2,64,2]{5,4,3,2,1,0:T(8,128)} %reshape.809, f32[]{:T(128)} %constant.51.clone.1), dimensions={1,3,5}, to_apply=%region_4.5 | reduce | flops 57344 | bytes 294916 | tf_op jit(solution)/shard_map/reduce_sum | solution.py:49
  225.4 1.9 collective-permute-start.4
  227.3 7.6 %collective-permute-start.5 = (bf16[1,1,32,64]{3,2,1,0:T(8,128)(2,1)S(1)}, bf16[1,1,32,64]{3,2,1,0:T(8,128)(2,1)S(1)}, u32[]{:S(2)}, u32[]{:S(2)}) collective-permute-start(bf16[1,1,32,64]{3,2,1,0:T(8,128)(2,1)S(1)} %get-tuple-element.91), channel_id=1, source_target_pairs={{8,0},{16,8},{24,16},{32,24},{40,32},{48,40},{56,48},{64,56},{72,6... | collective-permute-start | bytes 12296 | tf_op jit(solution)/shard_map/ppermute | solution.py:24
  235.0 1.3 collective-permute-done.5
  236.4 2.1 reshape.810
  238.6 0.2 reduce_sum.61
  239.0 1.9 collective-permute-start.6
  240.9 7.5 %collective-permute-start.7 = (bf16[1,1,16,32]{3,2,1,0:T(8,128)(2,1)S(1)}, bf16[1,1,16,32]{3,2,1,0:T(8,128)(2,1)S(1)}, u32[]{:S(2)}, u32[]{:S(2)}) collective-permute-start(bf16[1,1,16,32]{3,2,1,0:T(8,128)(2,1)S(1)} %get-tuple-element.116), channel_id=1, source_target_pairs={{8,0},{16,8},{24,16},{32,24},{40,32},{48,40},{56,48},{64,56},{72,6... | collective-permute-start | bytes 3080 | tf_op jit(solution)/shard_map/ppermute | solution.py:24
  248.5 1.3 collective-permute-done.7
  250.2 7.5 %collective-permute-start.9 = (bf16[1,1,8,16]{3,2,1,0:T(8,128)(2,1)S(1)}, bf16[1,1,8,16]{3,2,1,0:T(8,128)(2,1)S(1)}, u32[]{:S(2)}, u32[]{:S(2)}) collective-permute-start(bf16[1,1,8,16]{3,2,1,0:T(8,128)(2,1)S(1)} %get-tuple-element.126), channel_id=1, source_target_pairs={{8,0},{16,8},{24,16},{32,24},{40,32},{48,40},{56,48},{64,56},{72,6... | collective-permute-start | bytes 776 | tf_op jit(solution)/shard_map/ppermute | solution.py:24
  257.7 1.9 collective-permute-start.8
  259.7 6.8 %collective-permute-done.8 = bf16[1,1,8,16]{3,2,1,0:T(8,128)(2,1)S(1)} collective-permute-done((bf16[1,1,8,16]{3,2,1,0:T(8,128)(2,1)S(1)}, bf16[1,1,8,16]{3,2,1,0:T(8,128)(2,1)S(1)}, u32[]{:S(2)}, u32[]{:S(2)}) %collective-permute-start.8) | collective-permute-done | bytes 288 | tf_op jit(solution)/shard_map/ppermute | solution.py:21
  266.7 1.9 collective-permute-start.11
  268.7 3.9 collective-permute-start.10
  272.6 4.8 collective-permute-done.10
  277.9 1.9 collective-permute-start.12
  279.8 7.2 %collective-permute-start.13 = (bf16[1,1,16,32]{3,2,1,0:T(8,128)(2,1)S(1)}, bf16[1,1,16,32]{3,2,1,0:T(8,128)(2,1)S(1)}, u32[]{:S(2)}, u32[]{:S(2)}) collective-permute-start(bf16[1,1,16,32]{3,2,1,0:T(8,128)(2,1)S(1)} %get-tuple-element.114), channel_id=1, source_target_pairs={{8,0},{16,8},{24,16},{32,24},{40,32},{48,40},{56,48},{64,56},{72,6... | collective-permute-start | bytes 3080 | tf_op jit(solution)/shard_map/ppermute | solution.py:24
  287.1 1.3 collective-permute-done.13
  289.0 1.9 collective-permute-start.14
  290.9 7.5 %collective-permute-start.15 = (bf16[1,1,32,64]{3,2,1,0:T(8,128)(2,1)S(1)}, bf16[1,1,32,64]{3,2,1,0:T(8,128)(2,1)S(1)}, u32[]{:S(2)}, u32[]{:S(2)}) collective-permute-start(bf16[1,1,32,64]{3,2,1,0:T(8,128)(2,1)S(1)} %get-tuple-element.89), channel_id=1, source_target_pairs={{8,0},{16,8},{24,16},{32,24},{40,32},{48,40},{56,48},{64,56},{72,6... | collective-permute-start | bytes 12296 | tf_op jit(solution)/shard_map/ppermute | solution.py:24
  298.5 1.2 collective-permute-done.15
  300.9 1.9 collective-permute-start.16
  302.8 7.7 %collective-permute-start.17 = (bf16[1,1,64,128]{2,1,3,0:T(2,128)(2,1)S(1)}, bf16[1,1,64,128]{2,1,3,0:T(2,128)(2,1)S(1)}, u32[]{:S(2)}, u32[]{:S(2)}) collective-permute-start(bf16[1,1,64,128]{2,1,3,0:T(2,128)(2,1)S(1)} %get-tuple-element.57), channel_id=1, source_target_pairs={{8,0},{16,8},{24,16},{32,24},{40,32},{48,40},{56,48},{64,56},{72,6... | collective-permute-start | bytes 49160 | tf_op jit(solution)/shard_map/ppermute | solution.py:24
  310.6 1.8 collective-permute-done.17
  312.4 0.3 maximum_convert_fusion.1
  312.7 0.6 fusion.97
  313.5 0.8 reshape.813
  314.4 25.8 %all-gather.3.cloned.1.call-done = bf16[8,1,65536]{2,1,0:T(2,128)(2,1)} async-done(((bf16[1,1,65536]{2,1,0:T(2,128)(2,1)}), bf16[8,1,65536]{2,1,0:T(2,128)(2,1)}) %all-gather.3.cloned.1.call-update) | async-done | bytes 1048592 | tf_op jit(solution)/shard_map/all_gather | solution.py:101
  340.2 2.9 fusion
  343.1 0.9 copy.151
  344.0 144.2 %psum.23 = f32[1,8]{1,0:T(1,128)S(1)} all-reduce(f32[1,8]{1,0:T(1,128)S(1)} %fusion), channel_id=1, replica_groups=mesh['grid'=64,'state'=8] {'grid'}, use_global_device_ids=true, to_apply=%region_8.9 | all-reduce | flops 8 | bytes 64 | tf_op jit(solution)/shard_map/psum | solution.py:104
  488.2 0.5 broadcast_multiply_fusion.1
  (99 shorter events, 4.6 us)
Async XLA Ops:
  7.2 333.0 %all-gather.3.cloned.1.call-start = ((), (), s32[]{:S(2)}) async-start(), calls=%async_computation | async-start | bytes 2359296 | tf_op jit(solution)/shard_map/all_gather | solution.py:101
  8.7 25.6 %collective-permute-start.1 = (f32[1,2,64,128]{3,2,1,0:T(8,128)S(1)}, f32[1,2,64,128]{3,2,1,0:T(8,128)S(1)}, u32[]{:S(2)}, u32[]{:S(2)}) collective-permute-start(f32[1,2,64,128]{3,2,1,0:T(8,128)S(1)} %get-tuple-element.63), channel_id=1, source_target_pairs={{0,8},{8,16},{16,24},{24,32},{32,40},{40,48},{48,56},{56,64},{64,7... | collective-permute-start | bytes 196616 | tf_op jit(solution)/shard_map/ppermute | solution.py:21
  12.5 23.6 %collective-permute-start = (f32[1,2,64,128]{3,2,1,0:T(8,128)}, f32[1,2,64,128]{3,2,1,0:T(8,128)S(1)}, u32[]{:S(2)}, u32[]{:S(2)}) collective-permute-start(f32[1,2,64,128]{3,2,1,0:T(8,128)} %get-tuple-element.64), channel_id=1, source_target_pairs={{8,0},{16,8},{24,16},{32,24},{40,32},{48,40},{56,48},{64,56},{72,6... | collective-permute-start | bytes 196616 | tf_op jit(solution)/shard_map/ppermute | solution.py:24
  30.5 2.8 copy-start.1
  30.5 3.8 copy-start
  36.1 4.8 copy-start.2
  36.1 4.8 copy-start.3
  188.0 9.5 %collective-permute-start.2 = (bf16[1,1,64,128]{2,1,3,0:T(2,128)(2,1)S(1)}, bf16[1,1,64,128]{2,1,3,0:T(2,128)(2,1)S(1)}, u32[]{:S(2)}, u32[]{:S(2)}) collective-permute-start(bf16[1,1,64,128]{2,1,3,0:T(2,128)(2,1)S(1)} %get-tuple-element.58), channel_id=1, source_target_pairs={{0,8},{8,16},{16,24},{24,32},{32,40},{40,48},{48,56},{56,64},{64,7... | collective-permute-start | bytes 49160 | tf_op jit(solution)/shard_map/ppermute | solution.py:21
  190.0 9.1 %collective-permute-start.3 = (bf16[1,1,64,128]{2,1,3,0:T(2,128)(2,1)S(1)}, bf16[1,1,64,128]{2,1,3,0:T(2,128)(2,1)S(1)}, u32[]{:S(2)}, u32[]{:S(2)}) collective-permute-start(bf16[1,1,64,128]{2,1,3,0:T(2,128)(2,1)S(1)} %get-tuple-element.59), channel_id=1, source_target_pairs={{8,0},{16,8},{24,16},{32,24},{40,32},{48,40},{56,48},{64,56},{72,6... | collective-permute-start | bytes 49160 | tf_op jit(solution)/shard_map/ppermute | solution.py:24
  225.4 9.5 %collective-permute-start.4 = (bf16[1,1,32,64]{3,2,1,0:T(8,128)(2,1)S(1)}, bf16[1,1,32,64]{3,2,1,0:T(8,128)(2,1)S(1)}, u32[]{:S(2)}, u32[]{:S(2)}) collective-permute-start(bf16[1,1,32,64]{3,2,1,0:T(8,128)(2,1)S(1)} %get-tuple-element.90), channel_id=1, source_target_pairs={{0,8},{8,16},{16,24},{24,32},{32,40},{40,48},{48,56},{56,64},{64,7... | collective-permute-start | bytes 12296 | tf_op jit(solution)/shard_map/ppermute | solution.py:21
  227.3 8.9 %collective-permute-start.5 = (bf16[1,1,32,64]{3,2,1,0:T(8,128)(2,1)S(1)}, bf16[1,1,32,64]{3,2,1,0:T(8,128)(2,1)S(1)}, u32[]{:S(2)}, u32[]{:S(2)}) collective-permute-start(bf16[1,1,32,64]{3,2,1,0:T(8,128)(2,1)S(1)} %get-tuple-element.91), channel_id=1, source_target_pairs={{8,0},{16,8},{24,16},{32,24},{40,32},{48,40},{56,48},{64,56},{72,6... | collective-permute-start | bytes 12296 | tf_op jit(solution)/shard_map/ppermute | solution.py:24
  239.0 9.5 %collective-permute-start.6 = (bf16[1,1,16,32]{3,2,1,0:T(8,128)(2,1)S(1)}, bf16[1,1,16,32]{3,2,1,0:T(8,128)(2,1)S(1)}, u32[]{:S(2)}, u32[]{:S(2)}) collective-permute-start(bf16[1,1,16,32]{3,2,1,0:T(8,128)(2,1)S(1)} %get-tuple-element.115), channel_id=1, source_target_pairs={{0,8},{8,16},{16,24},{24,32},{32,40},{40,48},{48,56},{56,64},{64,7... | collective-permute-start | bytes 3080 | tf_op jit(solution)/shard_map/ppermute | solution.py:21
  240.9 8.8 %collective-permute-start.7 = (bf16[1,1,16,32]{3,2,1,0:T(8,128)(2,1)S(1)}, bf16[1,1,16,32]{3,2,1,0:T(8,128)(2,1)S(1)}, u32[]{:S(2)}, u32[]{:S(2)}) collective-permute-start(bf16[1,1,16,32]{3,2,1,0:T(8,128)(2,1)S(1)} %get-tuple-element.116), channel_id=1, source_target_pairs={{8,0},{16,8},{24,16},{32,24},{40,32},{48,40},{56,48},{64,56},{72,6... | collective-permute-start | bytes 3080 | tf_op jit(solution)/shard_map/ppermute | solution.py:24
  250.2 9.4 %collective-permute-start.9 = (bf16[1,1,8,16]{3,2,1,0:T(8,128)(2,1)S(1)}, bf16[1,1,8,16]{3,2,1,0:T(8,128)(2,1)S(1)}, u32[]{:S(2)}, u32[]{:S(2)}) collective-permute-start(bf16[1,1,8,16]{3,2,1,0:T(8,128)(2,1)S(1)} %get-tuple-element.126), channel_id=1, source_target_pairs={{8,0},{16,8},{24,16},{32,24},{40,32},{48,40},{56,48},{64,56},{72,6... | collective-permute-start | bytes 776 | tf_op jit(solution)/shard_map/ppermute | solution.py:24
  257.7 8.8 %collective-permute-start.8 = (bf16[1,1,8,16]{3,2,1,0:T(8,128)(2,1)S(1)}, bf16[1,1,8,16]{3,2,1,0:T(8,128)(2,1)S(1)}, u32[]{:S(2)}, u32[]{:S(2)}) collective-permute-start(bf16[1,1,8,16]{3,2,1,0:T(8,128)(2,1)S(1)} %get-tuple-element.126), channel_id=1, source_target_pairs={{0,8},{8,16},{16,24},{24,32},{32,40},{40,48},{48,56},{56,64},{64,7... | collective-permute-start | bytes 776 | tf_op jit(solution)/shard_map/ppermute | solution.py:21
  266.7 5.9 %collective-permute-start.11 = (bf16[1,1,8,16]{3,2,1,0:T(8,128)(2,1)S(1)}, bf16[1,1,8,16]{3,2,1,0:T(8,128)(2,1)S(1)}, u32[]{:S(2)}, u32[]{:S(2)}) collective-permute-start(bf16[1,1,8,16]{3,2,1,0:T(8,128)(2,1)S(1)} %get-tuple-element.16), channel_id=1, source_target_pairs={{8,0},{16,8},{24,16},{32,24},{40,32},{48,40},{56,48},{64,56},{72,6... | collective-permute-start | bytes 776 | tf_op jit(solution)/shard_map/ppermute | solution.py:24
  268.7 8.8 %collective-permute-start.10 = (bf16[1,1,8,16]{3,2,1,0:T(8,128)(2,1)S(1)}, bf16[1,1,8,16]{3,2,1,0:T(8,128)(2,1)S(1)}, u32[]{:S(2)}, u32[]{:S(2)}) collective-permute-start(bf16[1,1,8,16]{3,2,1,0:T(8,128)(2,1)S(1)} %get-tuple-element.16), channel_id=1, source_target_pairs={{0,8},{8,16},{16,24},{24,32},{32,40},{40,48},{48,56},{56,64},{64,7... | collective-permute-start | bytes 776 | tf_op jit(solution)/shard_map/ppermute | solution.py:21
  277.9 9.2 %collective-permute-start.12 = (bf16[1,1,16,32]{3,2,1,0:T(8,128)(2,1)S(1)}, bf16[1,1,16,32]{3,2,1,0:T(8,128)(2,1)S(1)}, u32[]{:S(2)}, u32[]{:S(2)}) collective-permute-start(bf16[1,1,16,32]{3,2,1,0:T(8,128)(2,1)S(1)} %get-tuple-element.113), channel_id=1, source_target_pairs={{0,8},{8,16},{16,24},{24,32},{32,40},{40,48},{48,56},{56,64},{64,7... | collective-permute-start | bytes 3080 | tf_op jit(solution)/shard_map/ppermute | solution.py:21
  279.8 8.6 %collective-permute-start.13 = (bf16[1,1,16,32]{3,2,1,0:T(8,128)(2,1)S(1)}, bf16[1,1,16,32]{3,2,1,0:T(8,128)(2,1)S(1)}, u32[]{:S(2)}, u32[]{:S(2)}) collective-permute-start(bf16[1,1,16,32]{3,2,1,0:T(8,128)(2,1)S(1)} %get-tuple-element.114), channel_id=1, source_target_pairs={{8,0},{16,8},{24,16},{32,24},{40,32},{48,40},{56,48},{64,56},{72,6... | collective-permute-start | bytes 3080 | tf_op jit(solution)/shard_map/ppermute | solution.py:24
  289.0 9.6 %collective-permute-start.14 = (bf16[1,1,32,64]{3,2,1,0:T(8,128)(2,1)S(1)}, bf16[1,1,32,64]{3,2,1,0:T(8,128)(2,1)S(1)}, u32[]{:S(2)}, u32[]{:S(2)}) collective-permute-start(bf16[1,1,32,64]{3,2,1,0:T(8,128)(2,1)S(1)} %get-tuple-element.88), channel_id=1, source_target_pairs={{0,8},{8,16},{16,24},{24,32},{32,40},{40,48},{48,56},{56,64},{64,7... | collective-permute-start | bytes 12296 | tf_op jit(solution)/shard_map/ppermute | solution.py:21
  290.9 8.9 %collective-permute-start.15 = (bf16[1,1,32,64]{3,2,1,0:T(8,128)(2,1)S(1)}, bf16[1,1,32,64]{3,2,1,0:T(8,128)(2,1)S(1)}, u32[]{:S(2)}, u32[]{:S(2)}) collective-permute-start(bf16[1,1,32,64]{3,2,1,0:T(8,128)(2,1)S(1)} %get-tuple-element.89), channel_id=1, source_target_pairs={{8,0},{16,8},{24,16},{32,24},{40,32},{48,40},{56,48},{64,56},{72,6... | collective-permute-start | bytes 12296 | tf_op jit(solution)/shard_map/ppermute | solution.py:24
  300.9 9.8 %collective-permute-start.16 = (bf16[1,1,64,128]{2,1,3,0:T(2,128)(2,1)S(1)}, bf16[1,1,64,128]{2,1,3,0:T(2,128)(2,1)S(1)}, u32[]{:S(2)}, u32[]{:S(2)}) collective-permute-start(bf16[1,1,64,128]{2,1,3,0:T(2,128)(2,1)S(1)} %get-tuple-element.56), channel_id=1, source_target_pairs={{0,8},{8,16},{16,24},{24,32},{32,40},{40,48},{48,56},{56,64},{64,7... | collective-permute-start | bytes 49160 | tf_op jit(solution)/shard_map/ppermute | solution.py:21
  302.8 9.6 %collective-permute-start.17 = (bf16[1,1,64,128]{2,1,3,0:T(2,128)(2,1)S(1)}, bf16[1,1,64,128]{2,1,3,0:T(2,128)(2,1)S(1)}, u32[]{:S(2)}, u32[]{:S(2)}) collective-permute-start(bf16[1,1,64,128]{2,1,3,0:T(2,128)(2,1)S(1)} %get-tuple-element.57), channel_id=1, source_target_pairs={{8,0},{16,8},{24,16},{32,24},{40,32},{48,40},{56,48},{64,56},{72,6... | collective-permute-start | bytes 49160 | tf_op jit(solution)/shard_map/ppermute | solution.py:24
Sparse Core Ops, SparseCore 0:
  314.4 25.7 all-gather.2
where the time goes:
time: 496 us
  blocking collectives  285 us (57%)
  starting transfers between devices  87.3 us (18%)
  waiting for transfers between devices  46.3 us (9%)
  local copies, waits for them, and re-layouts  42.6 us (9%)
  between operations  16 us (3%)
  other arithmetic  15.5 us (3%)
    psum x1, blocking collectives, on_device(): summed = lax.psum(row_block, 'grid')  144 us
    psum x1, blocking collectives, on_device(): lax.psum((jnp.sum(orbitals * hpsi, axis=(1, 2, 3)), jnp.sum(orbitals * or...  141 us
    ppermute x9, starting transfers between devices, with_halo(): lax.ppermute(lax.slice_in_dim(block, 0, width, axis=dim), axis, backward)  66.1 us
    all_gather x1, waiting for transfers between devices, on_device(): lax.all_gather(rounded, 'state', axis=0, tiled=True)  25.8 us
    ppermute x9, starting transfers between devices, with_halo(): lax.ppermute(lax.slice_in_dim(block, block.shape[dim] - width, None, axis...  21.2 us
    reshape x2, local copies, waits for them, and re-layouts, restrict(): shaped = values.reshape(count, sx // 2, 2, sy // 2, 2, sz // 2, 2)  20.2 us
    ppermute x9, waiting for transfers between devices, with_halo(): lax.ppermute(lax.slice_in_dim(block, block.shape[dim] - width, None, axis...  12.1 us
  transfers between devices with their start and end apart: 19, of which 11 were waited for; matrix products, arithmetic and copies ran while one was open for 2% of the time, Pallas kernels for 0%

commit v1 on v0

--- a/solution.py
+++ b/solution.py
@@ -10,6 +10,11 @@
 FAR_COEF = -1.0 / 12.0
 SHIFT_TERM = 0.25
 DAMPING = 2.0 / 3.0
+
+
+def gather_over(x, axis, d):
+    stack = jnp.stack([x] * lax.axis_size(axis))
+    return jnp.concatenate(lax.all_to_all(stack, axis, 0, 0), axis=d)
 
 
 def with_halo(block, sides, width):
@@ -96,10 +101,7 @@
     count = corrections.shape[0]
     rounded = corrections.astype(jnp.bfloat16).reshape(count, -1)
     row_block = jnp.einsum(
-        "ac,bc->ab",
-        rounded,
-        lax.all_gather(rounded, "state", axis=0, tiled=True),
-        preferred_element_type=jnp.float32,
+        "ac,bc->ab", rounded, gather_over(rounded, "state", 0), preferred_element_type=jnp.float32
     )
     summed = lax.psum(row_block, "grid")
     correlation_gram = summed / jnp.float32(rounded.shape[1] * lax.axis_size("grid"))

time: 496 us -> 479 us (0.966)
  the two profiles are of different devices: /device:TPU:4 before, /device:TPU:2 now
where the time goes in v1:
time: 479 us; the launch traced here: 478 us
  blocking collectives  284 us (59%)
  starting transfers between devices  96 us (20%)
  local copies, waits for them, and re-layouts  45.2 us (9%)
  waiting for transfers between devices  25.4 us (5%)
  other arithmetic  23.3 us (5%)
    psum x1, blocking collectives, on_device(): summed = lax.psum(row_block, 'grid')  144 us
    psum x1, blocking collectives, on_device(): lax.psum((jnp.sum(orbitals * hpsi, axis=(1, 2, 3)), jnp.sum(orbitals * or...  141 us
    ppermute x9, starting transfers between devices, with_halo(): lax.ppermute(lax.slice_in_dim(block, 0, width, axis=dim), axis, backward)  72 us
    reshape x2, local copies, waits for them, and re-layouts, restrict(): shaped = values.reshape(count, sx // 2, 2, sy // 2, 2, sz // 2, 2)  20.2 us
    ppermute x9, starting transfers between devices, with_halo(): lax.ppermute(lax.slice_in_dim(block, block.shape[dim] - width, None, axis...  19.2 us
    all_to_all x1, waiting for transfers between devices, gather_over(): return jnp.concatenate(lax.all_to_all(stack, axis, 0, 0), axis=d)  14.3 us
    unnamed x20, local copies, waits for them, and re-layouts  12.7 us
    ppermute x9, waiting for transfers between devices, with_halo(): lax.ppermute(lax.slice_in_dim(block, 0, width, axis=dim), axis, backward)  10.6 us
  transfers between devices with their start and end apart: 19, of which 11 were waited for; matrix products, arithmetic and copies ran while one was open for 2% of the time, Pallas kernels for 0%

profile of v1, /device:TPU:2, one launch (start us, length us, event | category | flops | bytes accessed | tf_op | source)
XLA Modules:
  0.0 478.1 jit_solution(10366700870898314755)
XLA Ops:
  0.6 0.9 fusion.122
  1.5 3.8 collective-permute-start.1
  5.4 11.9 %collective-permute-start = (f32[1,2,64,128]{3,2,1,0:T(8,128)S(1)}, f32[1,2,64,128]{3,2,1,0:T(8,128)S(1)}, u32[]{:S(2)}, u32[]{:S(2)}) collective-permute-start(f32[1,2,64,128]{3,2,1,0:T(8,128)S(1)} %get-tuple-element.64), channel_id=1, source_target_pairs={{8,0},{16,8},{24,16},{32,24},{40,32},{48,40},{56,48},{64,56},{72,6... | collective-permute-start | bytes 196616 | tf_op jit(solution)/shard_map/ppermute | solution.py:29
  17.3 1.2 copy.113
  18.5 1.1 fusion.112
  19.6 1.1 fusion.113
  20.7 1.0 fusion.115
  21.8 1.0 fusion.117
  22.8 0.3 copy.123
  23.1 0.3 copy.125
  23.4 0.3 copy.119
  23.9 1.0 copy.134
  24.9 0.7 multiply_reduce_fusion.1
  25.6 0.7 copy-done.2
  26.4 0.9 fusion.119
  27.2 1.9 copy.150
  29.2 1.9 copy.152
  31.2 1.0 copy.151
  32.2 1.0 copy.153
  33.2 4.4 multiply_reduce_fusion
  37.6 140.7 %all-reduce = (f32[1]{0:T(128)}, f32[1]{0:T(128)}) all-reduce(f32[1]{0:T(128)} %bitcast.1, f32[1]{0:T(128)} %bitcast.2), channel_id=1, replica_groups=mesh['grid'=64,'state'=8] {'grid'}, use_global_device_ids=true, to_apply=%region_1.2 | all-reduce | flops 2 | bytes 16 | tf_op jit(solution)/shard_map/psum | solution.py:94
  180.3 1.9 collective-permute-start.2
  182.2 7.2 %collective-permute-start.3 = (bf16[1,1,64,128]{2,1,3,0:T(2,128)(2,1)S(1)}, bf16[1,1,64,128]{2,1,3,0:T(2,128)(2,1)S(1)}, u32[]{:S(2)}, u32[]{:S(2)}) collective-permute-start(bf16[1,1,64,128]{2,1,3,0:T(2,128)(2,1)S(1)} %get-tuple-element.59), channel_id=1, source_target_pairs={{8,0},{16,8},{24,16},{32,24},{40,32},{48,40},{56,48},{64,56},{72,6... | collective-permute-start | bytes 49160 | tf_op jit(solution)/shard_map/ppermute | solution.py:29
  189.5 0.3 collective-permute-done.2
  189.8 1.6 collective-permute-done.3
  191.4 0.3 maximum_convert_fusion
  191.7 0.5 fusion.18
  192.4 18.1 %reshape.814 = f32[4,2,32,2,64,2]{5,4,3,2,1,0:T(8,128)} reshape(f32[1,8,64,128]{3,2,1,0:T(8,128)S(1)} %copy.138) | data formatting | bytes 524288 | tf_op jit(solution)/shard_map/reshape | solution.py:53
  210.5 7.0 %reduce_sum.60 = f32[4,32,64]{2,1,0:T(8,128)S(1)} reduce(f32[4,2,32,2,64,2]{5,4,3,2,1,0:T(8,128)} %reshape.814, f32[]{:T(128)} %constant.51.clone.1), dimensions={1,3,5}, to_apply=%region_4.5 | reduce | flops 57344 | bytes 294916 | tf_op jit(solution)/shard_map/reduce_sum | solution.py:54
  217.7 1.9 collective-permute-start.4
  219.6 7.6 %collective-permute-start.5 = (bf16[1,1,32,64]{3,2,1,0:T(8,128)(2,1)S(1)}, bf16[1,1,32,64]{3,2,1,0:T(8,128)(2,1)S(1)}, u32[]{:S(2)}, u32[]{:S(2)}) collective-permute-start(bf16[1,1,32,64]{3,2,1,0:T(8,128)(2,1)S(1)} %get-tuple-element.91), channel_id=1, source_target_pairs={{8,0},{16,8},{24,16},{32,24},{40,32},{48,40},{56,48},{64,56},{72,6... | collective-permute-start | bytes 12296 | tf_op jit(solution)/shard_map/ppermute | solution.py:29
  227.2 1.3 collective-permute-done.5
  228.7 2.2 reshape.815
  231.2 1.9 collective-permute-start.6
  233.2 7.5 %collective-permute-start.7 = (bf16[1,1,16,32]{3,2,1,0:T(8,128)(2,1)S(1)}, bf16[1,1,16,32]{3,2,1,0:T(8,128)(2,1)S(1)}, u32[]{:S(2)}, u32[]{:S(2)}) collective-permute-start(bf16[1,1,16,32]{3,2,1,0:T(8,128)(2,1)S(1)} %get-tuple-element.116), channel_id=1, source_target_pairs={{8,0},{16,8},{24,16},{32,24},{40,32},{48,40},{56,48},{64,56},{72,6... | collective-permute-start | bytes 3080 | tf_op jit(solution)/shard_map/ppermute | solution.py:29
  240.7 1.3 collective-permute-done.7
  242.3 1.9 collective-permute-start.8
  244.2 7.5 %collective-permute-start.9 = (bf16[1,1,8,16]{3,2,1,0:T(8,128)(2,1)S(1)}, bf16[1,1,8,16]{3,2,1,0:T(8,128)(2,1)S(1)}, u32[]{:S(2)}, u32[]{:S(2)}) collective-permute-start(bf16[1,1,8,16]{3,2,1,0:T(8,128)(2,1)S(1)} %get-tuple-element.126), channel_id=1, source_target_pairs={{8,0},{16,8},{24,16},{32,24},{40,32},{48,40},{56,48},{64,56},{72,6... | collective-permute-start | bytes 776 | tf_op jit(solution)/shard_map/ppermute | solution.py:29
  251.9 1.1 collective-permute-done.9
  253.1 1.9 collective-permute-start.10
  255.0 7.5 %collective-permute-start.11 = (bf16[1,1,8,16]{3,2,1,0:T(8,128)(2,1)S(1)}, bf16[1,1,8,16]{3,2,1,0:T(8,128)(2,1)S(1)}, u32[]{:S(2)}, u32[]{:S(2)}) collective-permute-start(bf16[1,1,8,16]{3,2,1,0:T(8,128)(2,1)S(1)} %get-tuple-element.16), channel_id=1, source_target_pairs={{8,0},{16,8},{24,16},{32,24},{40,32},{48,40},{56,48},{64,56},{72,6... | collective-permute-start | bytes 776 | tf_op jit(solution)/shard_map/ppermute | solution.py:29
  262.7 1.1 collective-permute-done.11
  264.3 1.9 collective-permute-start.12
  266.2 7.5 %collective-permute-start.13 = (bf16[1,1,16,32]{3,2,1,0:T(8,128)(2,1)S(1)}, bf16[1,1,16,32]{3,2,1,0:T(8,128)(2,1)S(1)}, u32[]{:S(2)}, u32[]{:S(2)}) collective-permute-start(bf16[1,1,16,32]{3,2,1,0:T(8,128)(2,1)S(1)} %get-tuple-element.114), channel_id=1, source_target_pairs={{8,0},{16,8},{24,16},{32,24},{40,32},{48,40},{56,48},{64,56},{72,6... | collective-permute-start | bytes 3080 | tf_op jit(solution)/shard_map/ppermute | solution.py:29
  273.7 1.3 collective-permute-done.13
  275.7 1.9 collective-permute-start.14
  277.6 7.5 %collective-permute-start.15 = (bf16[1,1,32,64]{3,2,1,0:T(8,128)(2,1)S(1)}, bf16[1,1,32,64]{3,2,1,0:T(8,128)(2,1)S(1)}, u32[]{:S(2)}, u32[]{:S(2)}) collective-permute-start(bf16[1,1,32,64]{3,2,1,0:T(8,128)(2,1)S(1)} %get-tuple-element.89), channel_id=1, source_target_pairs={{8,0},{16,8},{24,16},{32,24},{40,32},{48,40},{56,48},{64,56},{72,6... | collective-permute-start | bytes 12296 | tf_op jit(solution)/shard_map/ppermute | solution.py:29
  285.2 1.3 collective-permute-done.15
  287.6 1.9 collective-permute-start.16
  289.5 7.7 %collective-permute-start.17 = (bf16[1,1,64,128]{2,1,3,0:T(2,128)(2,1)S(1)}, bf16[1,1,64,128]{2,1,3,0:T(2,128)(2,1)S(1)}, u32[]{:S(2)}, u32[]{:S(2)}) collective-permute-start(bf16[1,1,64,128]{2,1,3,0:T(2,128)(2,1)S(1)} %get-tuple-element.57), channel_id=1, source_target_pairs={{8,0},{16,8},{24,16},{32,24},{40,32},{48,40},{56,48},{64,56},{72,6... | collective-permute-start | bytes 49160 | tf_op jit(solution)/shard_map/ppermute | solution.py:29
  297.4 1.6 collective-permute-done.17
  298.9 0.3 maximum_convert_fusion.1
  299.3 1.4 fusion.97
  300.8 1.1 stack.3
  301.9 0.5 broadcast.366
  302.4 7.0 %reduce.7 = bf16[8,65536]{1,0:T(8,128)(2,1)S(1)} reduce(bf16[8,1,65536]{2,1,0:T(2,128)(2,1)S(1)} %stack.3, bf16[]{:T(256)} %broadcast.366), dimensions={1}, to_apply=%stack.3.reduce_sub_computation | reduce | bytes 2097154 | tf_op jit(solution)/shard_map/stack | solution.py:16
  309.5 1.9 reshape.820
  311.4 4.8 %all-to-all-start = ((bf16[8,2,32768]{2,1,0:T(2,128)(2,1)}), bf16[8,2,32768]{2,1,0:T(2,128)(2,1)S(1)}, u32[]{:S(2)}, u32[]{:S(2)}) async-start(bf16[8,2,32768]{2,1,0:T(2,128)(2,1)} %reshape.820), calls=%async_computation | async-start | bytes 2097152 | tf_op jit(solution)/shard_map/all_to_all | solution.py:17
  316.3 14.3 %all-to-all-done = bf16[8,2,32768]{2,1,0:T(2,128)(2,1)S(1)} async-done(((bf16[8,2,32768]{2,1,0:T(2,128)(2,1)}), bf16[8,2,32768]{2,1,0:T(2,128)(2,1)S(1)}, u32[]{:S(2)}, u32[]{:S(2)}) %all-to-all-start) | async-done | bytes 1048608 | tf_op jit(solution)/shard_map/all_to_all | solution.py:17
  330.7 1.0 reshape.821
  331.7 1.3 fusion
  333.1 0.9 copy.148
  334.0 143.6 %psum.23 = f32[1,8]{1,0:T(1,128)S(1)} all-reduce(f32[1,8]{1,0:T(1,128)S(1)} %fusion), channel_id=1, replica_groups=mesh['grid'=64,'state'=8] {'grid'}, use_global_device_ids=true, to_apply=%region_8.9 | all-reduce | flops 8 | bytes 64 | tf_op jit(solution)/shard_map/psum | solution.py:106
  477.6 0.5 broadcast_multiply_fusion.1
  (104 shorter events, 5.2 us)
Async XLA Ops:
  1.5 23.4 %collective-permute-start.1 = (f32[1,2,64,128]{3,2,1,0:T(8,128)S(1)}, f32[1,2,64,128]{3,2,1,0:T(8,128)S(1)}, u32[]{:S(2)}, u32[]{:S(2)}) collective-permute-start(f32[1,2,64,128]{3,2,1,0:T(8,128)S(1)} %get-tuple-element.63), channel_id=1, source_target_pairs={{0,8},{8,16},{16,24},{24,32},{32,40},{40,48},{48,56},{56,64},{64,7... | collective-permute-start | bytes 196616 | tf_op jit(solution)/shard_map/ppermute | solution.py:26
  5.4 20.3 %collective-permute-start = (f32[1,2,64,128]{3,2,1,0:T(8,128)S(1)}, f32[1,2,64,128]{3,2,1,0:T(8,128)S(1)}, u32[]{:S(2)}, u32[]{:S(2)}) collective-permute-start(f32[1,2,64,128]{3,2,1,0:T(8,128)S(1)} %get-tuple-element.64), channel_id=1, source_target_pairs={{8,0},{16,8},{24,16},{32,24},{40,32},{48,40},{56,48},{64,56},{72,6... | collective-permute-start | bytes 196616 | tf_op jit(solution)/shard_map/ppermute | solution.py:29
  20.7 2.1 copy-start.1
  21.8 2.1 copy-start.4
  25.6 0.7 copy-start.2
  26.4 4.8 copy-start.3
  180.3 9.5 %collective-permute-start.2 = (bf16[1,1,64,128]{2,1,3,0:T(2,128)(2,1)S(1)}, bf16[1,1,64,128]{2,1,3,0:T(2,128)(2,1)S(1)}, u32[]{:S(2)}, u32[]{:S(2)}) collective-permute-start(bf16[1,1,64,128]{2,1,3,0:T(2,128)(2,1)S(1)} %get-tuple-element.58), channel_id=1, source_target_pairs={{0,8},{8,16},{16,24},{24,32},{32,40},{40,48},{48,56},{56,64},{64,7... | collective-permute-start | bytes 49160 | tf_op jit(solution)/shard_map/ppermute | solution.py:26
  182.2 9.1 %collective-permute-start.3 = (bf16[1,1,64,128]{2,1,3,0:T(2,128)(2,1)S(1)}, bf16[1,1,64,128]{2,1,3,0:T(2,128)(2,1)S(1)}, u32[]{:S(2)}, u32[]{:S(2)}) collective-permute-start(bf16[1,1,64,128]{2,1,3,0:T(2,128)(2,1)S(1)} %get-tuple-element.59), channel_id=1, source_target_pairs={{8,0},{16,8},{24,16},{32,24},{40,32},{48,40},{56,48},{64,56},{72,6... | collective-permute-start | bytes 49160 | tf_op jit(solution)/shard_map/ppermute | solution.py:29
  217.7 9.5 %collective-permute-start.4 = (bf16[1,1,32,64]{3,2,1,0:T(8,128)(2,1)S(1)}, bf16[1,1,32,64]{3,2,1,0:T(8,128)(2,1)S(1)}, u32[]{:S(2)}, u32[]{:S(2)}) collective-permute-start(bf16[1,1,32,64]{3,2,1,0:T(8,128)(2,1)S(1)} %get-tuple-element.90), channel_id=1, source_target_pairs={{0,8},{8,16},{16,24},{24,32},{32,40},{40,48},{48,56},{56,64},{64,7... | collective-permute-start | bytes 12296 | tf_op jit(solution)/shard_map/ppermute | solution.py:26
  219.6 8.9 %collective-permute-start.5 = (bf16[1,1,32,64]{3,2,1,0:T(8,128)(2,1)S(1)}, bf16[1,1,32,64]{3,2,1,0:T(8,128)(2,1)S(1)}, u32[]{:S(2)}, u32[]{:S(2)}) collective-permute-start(bf16[1,1,32,64]{3,2,1,0:T(8,128)(2,1)S(1)} %get-tuple-element.91), channel_id=1, source_target_pairs={{8,0},{16,8},{24,16},{32,24},{40,32},{48,40},{56,48},{64,56},{72,6... | collective-permute-start | bytes 12296 | tf_op jit(solution)/shard_map/ppermute | solution.py:29
  231.2 9.5 %collective-permute-start.6 = (bf16[1,1,16,32]{3,2,1,0:T(8,128)(2,1)S(1)}, bf16[1,1,16,32]{3,2,1,0:T(8,128)(2,1)S(1)}, u32[]{:S(2)}, u32[]{:S(2)}) collective-permute-start(bf16[1,1,16,32]{3,2,1,0:T(8,128)(2,1)S(1)} %get-tuple-element.115), channel_id=1, source_target_pairs={{0,8},{8,16},{16,24},{24,32},{32,40},{40,48},{48,56},{56,64},{64,7... | collective-permute-start | bytes 3080 | tf_op jit(solution)/shard_map/ppermute | solution.py:26
  233.2 8.8 %collective-permute-start.7 = (bf16[1,1,16,32]{3,2,1,0:T(8,128)(2,1)S(1)}, bf16[1,1,16,32]{3,2,1,0:T(8,128)(2,1)S(1)}, u32[]{:S(2)}, u32[]{:S(2)}) collective-permute-start(bf16[1,1,16,32]{3,2,1,0:T(8,128)(2,1)S(1)} %get-tuple-element.116), channel_id=1, source_target_pairs={{8,0},{16,8},{24,16},{32,24},{40,32},{48,40},{56,48},{64,56},{72,6... | collective-permute-start | bytes 3080 | tf_op jit(solution)/shard_map/ppermute | solution.py:29
  242.3 9.6 %collective-permute-start.8 = (bf16[1,1,8,16]{3,2,1,0:T(8,128)(2,1)S(1)}, bf16[1,1,8,16]{3,2,1,0:T(8,128)(2,1)S(1)}, u32[]{:S(2)}, u32[]{:S(2)}) collective-permute-start(bf16[1,1,8,16]{3,2,1,0:T(8,128)(2,1)S(1)} %get-tuple-element.126), channel_id=1, source_target_pairs={{0,8},{8,16},{16,24},{24,32},{32,40},{40,48},{48,56},{56,64},{64,7... | collective-permute-start | bytes 776 | tf_op jit(solution)/shard_map/ppermute | solution.py:26
  244.2 8.8 %collective-permute-start.9 = (bf16[1,1,8,16]{3,2,1,0:T(8,128)(2,1)S(1)}, bf16[1,1,8,16]{3,2,1,0:T(8,128)(2,1)S(1)}, u32[]{:S(2)}, u32[]{:S(2)}) collective-permute-start(bf16[1,1,8,16]{3,2,1,0:T(8,128)(2,1)S(1)} %get-tuple-element.126), channel_id=1, source_target_pairs={{8,0},{16,8},{24,16},{32,24},{40,32},{48,40},{56,48},{64,56},{72,6... | collective-permute-start | bytes 776 | tf_op jit(solution)/shard_map/ppermute | solution.py:29
  253.1 9.6 %collective-permute-start.10 = (bf16[1,1,8,16]{3,2,1,0:T(8,128)(2,1)S(1)}, bf16[1,1,8,16]{3,2,1,0:T(8,128)(2,1)S(1)}, u32[]{:S(2)}, u32[]{:S(2)}) collective-permute-start(bf16[1,1,8,16]{3,2,1,0:T(8,128)(2,1)S(1)} %get-tuple-element.16), channel_id=1, source_target_pairs={{0,8},{8,16},{16,24},{24,32},{32,40},{40,48},{48,56},{56,64},{64,7... | collective-permute-start | bytes 776 | tf_op jit(solution)/shard_map/ppermute | solution.py:26
  255.0 8.8 %collective-permute-start.11 = (bf16[1,1,8,16]{3,2,1,0:T(8,128)(2,1)S(1)}, bf16[1,1,8,16]{3,2,1,0:T(8,128)(2,1)S(1)}, u32[]{:S(2)}, u32[]{:S(2)}) collective-permute-start(bf16[1,1,8,16]{3,2,1,0:T(8,128)(2,1)S(1)} %get-tuple-element.16), channel_id=1, source_target_pairs={{8,0},{16,8},{24,16},{32,24},{40,32},{48,40},{56,48},{64,56},{72,6... | collective-permute-start | bytes 776 | tf_op jit(solution)/shard_map/ppermute | solution.py:29
  264.3 9.4 %collective-permute-start.12 = (bf16[1,1,16,32]{3,2,1,0:T(8,128)(2,1)S(1)}, bf16[1,1,16,32]{3,2,1,0:T(8,128)(2,1)S(1)}, u32[]{:S(2)}, u32[]{:S(2)}) collective-permute-start(bf16[1,1,16,32]{3,2,1,0:T(8,128)(2,1)S(1)} %get-tuple-element.113), channel_id=1, source_target_pairs={{0,8},{8,16},{16,24},{24,32},{32,40},{40,48},{48,56},{56,64},{64,7... | collective-permute-start | bytes 3080 | tf_op jit(solution)/shard_map/ppermute | solution.py:26
  266.2 8.8 %collective-permute-start.13 = (bf16[1,1,16,32]{3,2,1,0:T(8,128)(2,1)S(1)}, bf16[1,1,16,32]{3,2,1,0:T(8,128)(2,1)S(1)}, u32[]{:S(2)}, u32[]{:S(2)}) collective-permute-start(bf16[1,1,16,32]{3,2,1,0:T(8,128)(2,1)S(1)} %get-tuple-element.114), channel_id=1, source_target_pairs={{8,0},{16,8},{24,16},{32,24},{40,32},{48,40},{56,48},{64,56},{72,6... | collective-permute-start | bytes 3080 | tf_op jit(solution)/shard_map/ppermute | solution.py:29
  275.7 9.5 %collective-permute-start.14 = (bf16[1,1,32,64]{3,2,1,0:T(8,128)(2,1)S(1)}, bf16[1,1,32,64]{3,2,1,0:T(8,128)(2,1)S(1)}, u32[]{:S(2)}, u32[]{:S(2)}) collective-permute-start(bf16[1,1,32,64]{3,2,1,0:T(8,128)(2,1)S(1)} %get-tuple-element.88), channel_id=1, source_target_pairs={{0,8},{8,16},{16,24},{24,32},{32,40},{40,48},{48,56},{56,64},{64,7... | collective-permute-start | bytes 12296 | tf_op jit(solution)/shard_map/ppermute | solution.py:26
  277.6 8.9 %collective-permute-start.15 = (bf16[1,1,32,64]{3,2,1,0:T(8,128)(2,1)S(1)}, bf16[1,1,32,64]{3,2,1,0:T(8,128)(2,1)S(1)}, u32[]{:S(2)}, u32[]{:S(2)}) collective-permute-start(bf16[1,1,32,64]{3,2,1,0:T(8,128)(2,1)S(1)} %get-tuple-element.89), channel_id=1, source_target_pairs={{8,0},{16,8},{24,16},{32,24},{40,32},{48,40},{56,48},{64,56},{72,6... | collective-permute-start | bytes 12296 | tf_op jit(solution)/shard_map/ppermute | solution.py:29
  287.6 9.8 %collective-permute-start.16 = (bf16[1,1,64,128]{2,1,3,0:T(2,128)(2,1)S(1)}, bf16[1,1,64,128]{2,1,3,0:T(2,128)(2,1)S(1)}, u32[]{:S(2)}, u32[]{:S(2)}) collective-permute-start(bf16[1,1,64,128]{2,1,3,0:T(2,128)(2,1)S(1)} %get-tuple-element.56), channel_id=1, source_target_pairs={{0,8},{8,16},{16,24},{24,32},{32,40},{40,48},{48,56},{56,64},{64,7... | collective-permute-start | bytes 49160 | tf_op jit(solution)/shard_map/ppermute | solution.py:26
  289.5 9.4 %collective-permute-start.17 = (bf16[1,1,64,128]{2,1,3,0:T(2,128)(2,1)S(1)}, bf16[1,1,64,128]{2,1,3,0:T(2,128)(2,1)S(1)}, u32[]{:S(2)}, u32[]{:S(2)}) collective-permute-start(bf16[1,1,64,128]{2,1,3,0:T(2,128)(2,1)S(1)} %get-tuple-element.57), channel_id=1, source_target_pairs={{8,0},{16,8},{24,16},{32,24},{40,32},{48,40},{56,48},{64,56},{72,6... | collective-permute-start | bytes 49160 | tf_op jit(solution)/shard_map/ppermute | solution.py:29
  311.4 19.3 %all-to-all-start = ((bf16[8,2,32768]{2,1,0:T(2,128)(2,1)}), bf16[8,2,32768]{2,1,0:T(2,128)(2,1)S(1)}, u32[]{:S(2)}, u32[]{:S(2)}) async-start(bf16[8,2,32768]{2,1,0:T(2,128)(2,1)} %reshape.820), calls=%async_computation | async-start | bytes 2097152 | tf_op jit(solution)/shard_map/all_to_all | solution.py:17
  331.7 1.3 copy-start
